TPU v7x, 32 devices: a whole 2x2x4 slice. The times are simulated.
32 devices in a mesh: gx: 4 (over z), gy: 2 (over x), gz: 4 (over y, core).
Axes of the slice: x: 2, y: 2, z: 4, core: 2. Of those that a mesh axis runs over, the one named last changes fastest.
Arguments:
- displacement: float32 [3, 32, 64, 512], P(None, 'gx', 'gy', 'gz'), may hold values from -0.1 to 0.1
- velocity: float32 [3, 32, 64, 512], P(None, 'gx', 'gy', 'gz'), may hold values from -1.55 to 1.55
- energy: float32 [32, 64, 512], P('gx', 'gy', 'gz'), may hold values from 1 to 4
- density: float32 [32, 64, 512], P('gx', 'gy', 'gz'), may hold values from 0.5 to 4
- region: int32 [32, 64, 512], P('gx', 'gy', 'gz'), may hold values from 0 to 10
- adiabatic: float32 [11], replicated, may hold values from 1.2 to 1.8
- face_flags: int32 [6], replicated, may hold values from 0 to 1
Outputs:
- final_displacement: float32 [3, 32, 64, 512], P(None, 'gx', 'gy', 'gz')
- final_velocity: float32 [3, 32, 64, 512], P(None, 'gx', 'gy', 'gz')
- final_energy: float32 [32, 64, 512], P('gx', 'gy', 'gz')
Inputs may be any that keep to these rules, and one draw needn't show every extreme that they name: `face_flags`: 1 marks a symmetry plane, 0 a free surface.
All inputs are finite; a program needn't handle non-finite values.
Results may differ from a plain program's by a relative error of at most 0.0003.
Values sent between devices are 32-bit elements; how exact they have to be, the bound alone decides.
A program may use at most 64 MiB of HBM per device.

v0:
```python
import jax
import jax.numpy as jnp
from jax import lax
from jax.sharding import PartitionSpec as P

STEPS = 2


COURANT = 0.25
QUAD_COEF = 1.0
LINEAR_COEF = 1.0
CORNERS = [
    (along_x, along_y, along_z) for along_x in (0, 1) for along_y in (0, 1) for along_z in (0, 1)
]


def passed_along(value, axis, steps):
    count = lax.axis_size(axis)
    first, last = (max(0, -steps), min(count, count - steps))
    return lax.ppermute(value, axis, [(source, source + steps) for source in range(first, last)])


def extended_2(block, sides, width):
    for axis, dim in sides:
        count = lax.axis_size(axis)
        forward = [(i, i + 1) for i in range(count - 1)]
        backward = [(target, source) for source, target in forward]
        low = lax.ppermute(
            lax.slice_in_dim(block, block.shape[dim] - width, None, axis=dim), axis, forward
        )
        high = lax.ppermute(lax.slice_in_dim(block, 0, width, axis=dim), axis, backward)
        block = jnp.concatenate([low, block, high], axis=dim)
    return block


def corner_views(extended, grid_shape):
    corner_sets = {}
    for offset in CORNERS:
        corner_sets[offset] = extended[
            :,
            offset[0] : offset[0] + grid_shape[0],
            offset[1] : offset[1] + grid_shape[1],
            offset[2] : offset[2] + grid_shape[2],
        ]
    return corner_sets


def spread(corner_sets, start_comp):
    result = []
    for direction in range(3):
        accum = 0.0
        for offset in CORNERS:
            if offset[direction] == 1:
                accum = accum + corner_sets[offset][start_comp : start_comp + 3]
            else:
                accum = accum - corner_sets[offset][start_comp : start_comp + 3]
        result.append(0.25 * accum)
    return result


def cofactors(matrix):

    def minor_det(row_one, row_two, col_one, col_two):
        return (
            matrix[row_one][col_one] * matrix[row_two][col_two]
            - matrix[row_one][col_two] * matrix[row_two][col_one]
        )

    return [
        [minor_det(1, 2, 1, 2), -minor_det(1, 2, 0, 2), minor_det(1, 2, 0, 1)],
        [-minor_det(0, 2, 1, 2), minor_det(0, 2, 0, 2), -minor_det(0, 2, 0, 1)],
        [minor_det(0, 1, 1, 2), -minor_det(0, 1, 0, 2), minor_det(0, 1, 0, 1)],
    ]


def kinematics(corner_sets):
    distorted = spread(corner_sets, 0)
    rate_terms = spread(corner_sets, 3)
    jacobian = [
        [
            distorted[direction][component] + (1.0 if component == direction else 0.0)
            for direction in range(3)
        ]
        for component in range(3)
    ]
    cofactor = cofactors(jacobian)
    volume = (
        jacobian[0][0] * cofactor[0][0]
        + jacobian[0][1] * cofactor[0][1]
        + jacobian[0][2] * cofactor[0][2]
    )
    change = 0.0
    for component in range(3):
        for direction in range(3):
            change = change + cofactor[component][direction] * rate_terms[direction][component]
    return (cofactor, volume, change / volume)


def minmod(forward, backward):
    return jnp.maximum(jnp.minimum(forward, backward), 0.0) + jnp.minimum(
        jnp.maximum(forward, backward), 0.0
    )


def face_ghosts(strain_rate, lower_rate, upper_rate, position, node_count, face_flags, dimension):
    lower_rate = jnp.where(
        position == 0, jnp.where(face_flags[2 * dimension] == 1, strain_rate, 0.0), lower_rate
    )
    upper_rate = jnp.where(
        position == node_count - 2,
        jnp.where(face_flags[2 * dimension + 1] == 1, strain_rate, 0.0),
        upper_rate,
    )
    return (lower_rate, upper_rate)


def stress(strain_rate, roughness, volume, density, energy, gamma_elem, present):
    dense_now = density / volume
    length = jnp.cbrt(volume)
    compress = jnp.maximum(-strain_rate, 0.0)
    viscous = jnp.where(
        present,
        dense_now * length * length * compress * (QUAD_COEF * compress + LINEAR_COEF * roughness),
        0.0,
    )
    pressure = (gamma_elem - 1.0) * dense_now * energy
    sound_sq = gamma_elem * (gamma_elem - 1.0) * energy
    total_stress = jnp.where(present, pressure + viscous, 0.0)
    step_ratio = jnp.where(present, length / jnp.sqrt(sound_sq + viscous / dense_now), jnp.inf)
    return (total_stress, dense_now, step_ratio)


def corner_force(cofactor, total_stress, offset):
    corner_signs = [2.0 * corner_bit - 1.0 for corner_bit in offset]
    return jnp.stack(
        [
            0.25
            * total_stress
            * (
                corner_signs[0] * cofactor[component][0]
                + corner_signs[1] * cofactor[component][1]
                + corner_signs[2] * cofactor[component][2]
            )
            for component in range(3)
        ]
    )


def node_sum(term_of):
    accum = None
    for offset in CORNERS:
        corner_term = term_of(offset)
        padded = jnp.pad(
            corner_term,
            (
                (0, 0),
                (offset[0], 1 - offset[0]),
                (offset[1], 1 - offset[1]),
                (offset[2], 1 - offset[2]),
            ),
        )
        accum = padded if accum is None else accum + padded
    return accum


def apply_walls(speeds, indices, counts, face_flags):
    components = []
    for dimension in range(3):
        on_wall = (indices[dimension] == 0) & (face_flags[2 * dimension] == 1) | (
            indices[dimension] == counts[dimension] - 1
        ) & (face_flags[2 * dimension + 1] == 1)
        components.append(jnp.where(on_wall, 0.0, speeds[dimension]))
    return jnp.stack(components)


def ghost_nodes(fields):
    arrived = passed_along(fields[:, :1], "gx", -1)
    fields = jnp.concatenate([fields, arrived], 1)
    arrived = passed_along(fields[:, :, :1], "gy", -1)
    fields = jnp.concatenate([fields, arrived], 2)
    arrived = passed_along(fields[:, :, :, :1], "gz", -1)
    return jnp.concatenate([fields, arrived], 3)


def fold_nodes(partial_value):
    incoming = passed_along(partial_value[:, -1:], "gx", 1)
    partial_value = jnp.concatenate([partial_value[:, :1] + incoming, partial_value[:, 1:-1]], 1)
    incoming = passed_along(partial_value[:, :, -1:], "gy", 1)
    partial_value = jnp.concatenate(
        [partial_value[:, :, :1] + incoming, partial_value[:, :, 1:-1]], 2
    )
    incoming = passed_along(partial_value[:, :, :, -1:], "gz", 1)
    return jnp.concatenate([partial_value[:, :, :, :1] + incoming, partial_value[:, :, :, 1:-1]], 3)


def body(displacement, velocity, energy, density, region, adiabatic, face_flags):
    grid_shape = energy.shape
    counts = (
        grid_shape[0] * lax.axis_size("gx"),
        grid_shape[1] * lax.axis_size("gy"),
        grid_shape[2] * lax.axis_size("gz"),
    )
    starts = (
        lax.axis_index("gx") * grid_shape[0],
        lax.axis_index("gy") * grid_shape[1],
        lax.axis_index("gz") * grid_shape[2],
    )
    indices = [
        (starts[0] + jnp.arange(grid_shape[0], dtype=jnp.int32))[:, None, None],
        (starts[1] + jnp.arange(grid_shape[1], dtype=jnp.int32))[None, :, None],
        (starts[2] + jnp.arange(grid_shape[2], dtype=jnp.int32))[None, None, :],
    ]
    present = (
        (indices[0] < counts[0] - 1) & (indices[1] < counts[1] - 1) & (indices[2] < counts[2] - 1)
    )
    region_ids = jnp.arange(adiabatic.shape[0], dtype=jnp.int32)[:, None, None, None]
    gamma_elem = jnp.sum(
        jnp.where(region[None] == region_ids, adiabatic[:, None, None, None], 0.0), 0
    )
    mass_term = jnp.where(present, 0.125 * density, 0.0)[None]
    node_mass = None
    for step_index in range(STEPS):
        extended = ghost_nodes(jnp.concatenate([displacement, velocity], 0))
        cofactor, volume, strain_rate = kinematics(corner_views(extended, grid_shape))
        framed = extended_2(strain_rate, (("gx", 0), ("gy", 1), ("gz", 2)), 1)
        lowers = [framed[:-2, 1:-1, 1:-1], framed[1:-1, :-2, 1:-1], framed[1:-1, 1:-1, :-2]]
        uppers = [framed[2:, 1:-1, 1:-1], framed[1:-1, 2:, 1:-1], framed[1:-1, 1:-1, 2:]]
        roughness = 0.0
        for dimension in range(3):
            lower_rate, upper_rate = face_ghosts(
                strain_rate,
                lowers[dimension],
                uppers[dimension],
                indices[dimension],
                counts[dimension],
                face_flags,
                dimension,
            )
            roughness = roughness + jnp.abs(
                minmod(upper_rate - strain_rate, strain_rate - lower_rate)
            )
        total_stress, dense_now, step_ratio = stress(
            strain_rate, roughness, volume, density, energy, gamma_elem, present
        )
        time_step = COURANT * lax.pmin(jnp.min(step_ratio), ("gx", "gy", "gz"))
        if node_mass is None:
            node_total = fold_nodes(
                node_sum(
                    lambda offset: jnp.concatenate(
                        [corner_force(cofactor, total_stress, offset), mass_term], 0
                    )
                )
            )
            force = node_total[:3]
            node_mass = node_total[3]
        else:
            force = fold_nodes(
                node_sum(lambda offset: corner_force(cofactor, total_stress, offset))
            )
        velocity = apply_walls(
            velocity + time_step * force / node_mass, indices, counts, face_flags
        )
        displacement = displacement + time_step * velocity
        energy = jnp.where(
            present, energy - time_step * total_stress * strain_rate / dense_now, energy
        )
    return (displacement, velocity, energy)


def solution(mesh):
    placed = (
        P(None, "gx", "gy", "gz"),
        P(None, "gx", "gy", "gz"),
        P("gx", "gy", "gz"),
        P("gx", "gy", "gz"),
        P("gx", "gy", "gz"),
        P(),
        P(),
    )
    return jax.shard_map(
        body,
        mesh=mesh,
        in_specs=placed,
        out_specs=(P(None, "gx", "gy", "gz"), P(None, "gx", "gy", "gz"), P("gx", "gy", "gz")),
        check_vma=False,
    )
```

profile of v0, /device:TPU:14, one launch (start us, length us, event | category | flops | bytes accessed | tf_op | source)
XLA Modules:
  0.0 223.2 jit_solution(6780053600067627661)
XLA Ops:
  2.8 2.4 %collective-permute-start = (f32[6,1,32,128]{3,2,1,0:T(8,128)S(1)}, f32[6,1,32,128]{3,2,1,0:T(8,128)S(1)}, u32[]{:S(2)}, u32[]{:S(2)}) collective-permute-start(f32[6,1,32,128]{3,2,1,0:T(8,128)S(1)} %slice.632), channel_id=1, source_target_pairs={{8,0},{16,8},{24,16},{9,1},{17,9},{25,17},{10,2},{18,10},{26,18},{... | collective-permute-start | bytes 294920 | tf_op jit(solution)/shard_map/ppermute | solution.py:20
  6.2 3.1 %collective-permute-done = f32[6,1,32,128]{3,2,1,0:T(8,128)S(1)} collective-permute-done((f32[6,1,32,128]{3,2,1,0:T(8,128)S(1)}, f32[6,1,32,128]{3,2,1,0:T(8,128)S(1)}, u32[]{:S(2)}, u32[]{:S(2)}) %collective-permute-start) | collective-permute-done | bytes 98336 | tf_op jit(solution)/shard_map/ppermute | solution.py:20
  9.3 2.4 %collective-permute-start.1 = (f32[6,9,1,128]{3,2,1,0:T(1,128)S(1)}, f32[6,9,1,128]{3,2,1,0:T(1,128)S(1)}, u32[]{:S(2)}, u32[]{:S(2)}) collective-permute-start(f32[6,9,1,128]{3,2,1,0:T(1,128)S(1)} %pad_maximum_fusion.66), channel_id=1, source_target_pairs={{4,0},{5,1},{6,2},{7,3},{12,8},{13,9},{14,10},{15,11},{20,16},{21,... | collective-permute-start | bytes 82952 | tf_op jit(solution)/shard_map/ppermute | solution.py:20
  11.8 1.5 collective-permute-done.1
  13.9 1.9 collective-permute-start.2
  15.8 1.5 collective-permute-done.2
  17.3 1.5 copy.43
  18.8 1.5 pad_maximum_fusion
  22.7 3.6 %collective-permute-start.4 = (f32[1,32,128]{2,1,0:T(8,128)S(1)}, f32[1,32,128]{2,1,0:T(8,128)S(1)}, u32[]{:S(2)}, u32[]{:S(2)}) collective-permute-start(f32[1,32,128]{2,1,0:T(8,128)S(1)} %get-tuple-element.155), channel_id=1, source_target_pairs={{0,8},{8,16},{16,24},{1,9},{9,17},{17,25},{2,10},{10,18},{18,26},{... | collective-permute-start | bytes 49160 | tf_op jit(solution)/shard_map/ppermute | solution.py:28
  26.3 2.4 %collective-permute-start.3 = (f32[1,32,128]{2,1,0:T(8,128)S(1)}, f32[1,32,128]{2,1,0:T(8,128)S(1)}, u32[]{:S(2)}, u32[]{:S(2)}) collective-permute-start(f32[1,32,128]{2,1,0:T(8,128)S(1)} %get-tuple-element.156), channel_id=1, source_target_pairs={{8,0},{16,8},{24,16},{9,1},{17,9},{25,17},{10,2},{18,10},{26,18},{... | collective-permute-start | bytes 49160 | tf_op jit(solution)/shard_map/ppermute | solution.py:31
  28.7 3.2 %collective-permute-done.3 = f32[1,32,128]{2,1,0:T(8,128)S(1)} collective-permute-done((f32[1,32,128]{2,1,0:T(8,128)S(1)}, f32[1,32,128]{2,1,0:T(8,128)S(1)}, u32[]{:S(2)}, u32[]{:S(2)}) %collective-permute-start.3) | collective-permute-done | bytes 16416 | tf_op jit(solution)/shard_map/ppermute | solution.py:31
  32.0 1.3 collective-permute-start.6
  33.3 4.5 %collective-permute-start.5 = (f32[10,1,128]{2,1,0:T(1,128)S(1)}, f32[10,1,128]{2,1,0:T(1,128)S(1)}, u32[]{:S(2)}, u32[]{:S(2)}) collective-permute-start(f32[10,1,128]{2,1,0:T(1,128)S(1)} %get-tuple-element.113), channel_id=1, source_target_pairs={{4,0},{5,1},{6,2},{7,3},{12,8},{13,9},{14,10},{15,11},{20,16},{21,... | collective-permute-start | bytes 15368 | tf_op jit(solution)/shard_map/ppermute | solution.py:31
  39.3 1.9 collective-permute-start.7
  41.2 2.4 %collective-permute-start.8 = (f32[10,34,1]{2,1,0:T(8,128)S(1)}, f32[10,34,1]{2,1,0:T(8,128)S(1)}, u32[]{:S(2)}, u32[]{:S(2)}) collective-permute-start(f32[10,34,1]{2,1,0:T(8,128)S(1)} %get-tuple-element.109), channel_id=1, source_target_pairs={{0,1},{1,2},{2,3},{4,5},{5,6},{6,7},{8,9},{9,10},{10,11},{12,13},{... | collective-permute-start | bytes 4088 | tf_op jit(solution)/shard_map/ppermute | solution.py:28
  46.1 2.2 collective-permute-done.8
  48.3 1.2 fusion.28
  50.6 1.3 pad_add_fusion
  52.0 1.9 collective-permute-start.9
  54.3 4.8 %collective-permute-done.9 = f32[4,1,33,129]{3,2,1,0:T(8,128)S(1)} collective-permute-done((f32[4,1,33,129]{3,2,1,0:T(8,128)S(1)}, f32[4,1,33,129]{3,2,1,0:T(8,128)S(1)}, u32[]{:S(2)}, u32[]{:S(2)}) %collective-permute-start.9) | collective-permute-done | bytes 68144 | tf_op jit(solution)/shard_map/ppermute | solution.py:20
  59.4 1.3 collective-permute-start.10
  61.2 3.9 %collective-permute-done.10 = f32[4,8,1,129]{3,1,2,0:T(8,128)S(1)} collective-permute-done((f32[4,8,1,129]{3,1,2,0:T(8,128)S(1)}, f32[4,8,1,129]{3,1,2,0:T(8,128)S(1)}, u32[]{:S(2)}, u32[]{:S(2)}) %collective-permute-start.10) | collective-permute-done | bytes 16544 | tf_op jit(solution)/shard_map/ppermute | solution.py:20
  65.3 1.9 collective-permute-start.11
  67.3 38.9 %pmin.14 = f32[]{:T(128)} all-reduce(f32[]{:T(128)} %get-tuple-element.26), channel_id=1, replica_groups=mesh['gx'=4,'gy'=2,'gz'=4] {'gx','gy','gz'}, use_global_device_ids=true, to_apply=%region_2.3 | all-reduce | flops 1 | bytes 8 | tf_op jit(solution)/shard_map/pmin | solution.py:245
  107.7 3.5 %collective-permute-start.12 = (f32[6,1,32,128]{3,2,1,0:T(8,128)S(1)}, f32[6,1,32,128]{3,2,1,0:T(8,128)S(1)}, u32[]{:S(2)}, u32[]{:S(2)}) collective-permute-start(f32[6,1,32,128]{3,2,1,0:T(8,128)S(1)} %pad_maximum_fusion.61), channel_id=1, source_target_pairs={{8,0},{16,8},{24,16},{9,1},{17,9},{25,17},{10,2},{18,10},{26,18},{... | collective-permute-start | bytes 294920 | tf_op jit(solution)/shard_map/ppermute | solution.py:20
  111.2 3.0 %collective-permute-done.12 = f32[6,1,32,128]{3,2,1,0:T(8,128)S(1)} collective-permute-done((f32[6,1,32,128]{3,2,1,0:T(8,128)S(1)}, f32[6,1,32,128]{3,2,1,0:T(8,128)S(1)}, u32[]{:S(2)}, u32[]{:S(2)}) %collective-permute-start.12) | collective-permute-done | bytes 98336 | tf_op jit(solution)/shard_map/ppermute | solution.py:20
  114.2 3.4 %collective-permute-start.13 = (f32[6,9,1,128]{3,2,1,0:T(1,128)S(1)}, f32[6,9,1,128]{3,2,1,0:T(1,128)S(1)}, u32[]{:S(2)}, u32[]{:S(2)}) collective-permute-start(f32[6,9,1,128]{3,2,1,0:T(1,128)S(1)} %pad_maximum_fusion.65), channel_id=1, source_target_pairs={{4,0},{5,1},{6,2},{7,3},{12,8},{13,9},{14,10},{15,11},{20,16},{21,... | collective-permute-start | bytes 82952 | tf_op jit(solution)/shard_map/ppermute | solution.py:20
  117.6 1.5 collective-permute-done.13
  119.7 2.1 collective-permute-start.14
  121.8 1.3 collective-permute-done.14
  126.8 2.7 %collective-permute-start.16 = (f32[1,32,128]{2,1,0:T(8,128)S(1)}, f32[1,32,128]{2,1,0:T(8,128)S(1)}, u32[]{:S(2)}, u32[]{:S(2)}) collective-permute-start(f32[1,32,128]{2,1,0:T(8,128)S(1)} %get-tuple-element.130), channel_id=1, source_target_pairs={{0,8},{8,16},{16,24},{1,9},{9,17},{17,25},{2,10},{10,18},{18,26},{... | collective-permute-start | bytes 49160 | tf_op jit(solution)/shard_map/ppermute | solution.py:28
  129.5 3.3 %collective-permute-start.15 = (f32[1,32,128]{2,1,0:T(8,128)S(1)}, f32[1,32,128]{2,1,0:T(8,128)S(1)}, u32[]{:S(2)}, u32[]{:S(2)}) collective-permute-start(f32[1,32,128]{2,1,0:T(8,128)S(1)} %get-tuple-element.131), channel_id=1, source_target_pairs={{8,0},{16,8},{24,16},{9,1},{17,9},{25,17},{10,2},{18,10},{26,18},{... | collective-permute-start | bytes 49160 | tf_op jit(solution)/shard_map/ppermute | solution.py:31
  132.8 2.3 %collective-permute-done.15 = f32[1,32,128]{2,1,0:T(8,128)S(1)} collective-permute-done((f32[1,32,128]{2,1,0:T(8,128)S(1)}, f32[1,32,128]{2,1,0:T(8,128)S(1)}, u32[]{:S(2)}, u32[]{:S(2)}) %collective-permute-start.15) | collective-permute-done | bytes 16416 | tf_op jit(solution)/shard_map/ppermute | solution.py:31
  135.1 1.3 collective-permute-start.18
  136.4 4.5 %collective-permute-start.17 = (f32[10,1,128]{2,1,0:T(1,128)S(1)}, f32[10,1,128]{2,1,0:T(1,128)S(1)}, u32[]{:S(2)}, u32[]{:S(2)}) collective-permute-start(f32[10,1,128]{2,1,0:T(1,128)S(1)} %get-tuple-element.111), channel_id=1, source_target_pairs={{4,0},{5,1},{6,2},{7,3},{12,8},{13,9},{14,10},{15,11},{20,16},{21,... | collective-permute-start | bytes 15368 | tf_op jit(solution)/shard_map/ppermute | solution.py:31
  141.0 1.3 collective-permute-done.17
  142.5 1.9 collective-permute-start.19
  144.4 2.4 %collective-permute-start.20 = (f32[10,34,1]{2,1,0:T(8,128)S(1)}, f32[10,34,1]{2,1,0:T(8,128)S(1)}, u32[]{:S(2)}, u32[]{:S(2)}) collective-permute-start(f32[10,34,1]{2,1,0:T(8,128)S(1)} %get-tuple-element.107), channel_id=1, source_target_pairs={{0,1},{1,2},{2,3},{4,5},{5,6},{6,7},{8,9},{9,10},{10,11},{12,13},{... | collective-permute-start | bytes 4088 | tf_op jit(solution)/shard_map/ppermute | solution.py:28
  147.6 3.8 %collective-permute-done.20 = f32[10,34,1]{2,1,0:T(8,128)S(1)} collective-permute-done((f32[10,34,1]{2,1,0:T(8,128)S(1)}, f32[10,34,1]{2,1,0:T(8,128)S(1)}, u32[]{:S(2)}, u32[]{:S(2)}) %collective-permute-start.20) | collective-permute-done | bytes 1392 | tf_op jit(solution)/shard_map/ppermute | solution.py:28
  151.6 1.2 fusion.30
  152.7 42.0 %pmin.15 = f32[]{:T(128)} all-reduce(f32[]{:T(128)} %get-tuple-element.8), channel_id=1, replica_groups=mesh['gx'=4,'gy'=2,'gz'=4] {'gx','gy','gz'}, use_global_device_ids=true, to_apply=%region_4.5 | all-reduce | flops 1 | bytes 8 | tf_op jit(solution)/shard_map/pmin | solution.py:245
  196.6 2.8 %fusion = f32[3,9,33,129]{3,2,1,0:T(8,128)S(1)} fusion(f32[1,8,32,128]{3,2,1,0:T(8,128)S(1)} %get-tuple-element.122, f32[1,8,32,128]{3,2,1,0:T(8,128)S(1)} %get-tuple-element.55, f32[1,8,32,128]{3,2,1,0:T(8,128)S(1)} %get-tuple-element.120, f32[1,8,32,128]{3,2,1,0:T(8,128)S(1)} %get-tuple-element.128, f32[1,8,32,128]{3,2,1,0:T(8,128)S(1)} %get-tuple-element.56, ...), kind=kLoop, calls=%fused_computation.18 | loop fusion | flops 12988107 | bytes 3605484 | tf_op jit(solution)/shard_map/add | solution.py:162
  199.4 2.6 %collective-permute-start.21 = (f32[3,1,33,129]{3,2,1,0:T(8,128)S(1)}, f32[3,1,33,129]{3,2,1,0:T(8,128)S(1)}, u32[]{:S(2)}, u32[]{:S(2)}) collective-permute-start(f32[3,1,33,129]{3,2,1,0:T(8,128)S(1)} %slice.716), channel_id=1, source_target_pairs={{0,8},{8,16},{16,24},{1,9},{9,17},{17,25},{2,10},{10,18},{18,26},{... | collective-permute-start | bytes 153260 | tf_op jit(solution)/shard_map/ppermute | solution.py:20
  202.3 3.9 %collective-permute-done.21 = f32[3,1,33,129]{3,2,1,0:T(8,128)S(1)} collective-permute-done((f32[3,1,33,129]{3,2,1,0:T(8,128)S(1)}, f32[3,1,33,129]{3,2,1,0:T(8,128)S(1)}, u32[]{:S(2)}, u32[]{:S(2)}) %collective-permute-start.21) | collective-permute-done | bytes 51116 | tf_op jit(solution)/shard_map/ppermute | solution.py:20
  206.4 1.3 collective-permute-start.22
  208.1 4.0 %collective-permute-done.22 = f32[3,8,1,129]{3,1,2,0:T(8,128)S(1)} collective-permute-done((f32[3,8,1,129]{3,1,2,0:T(8,128)S(1)}, f32[3,8,1,129]{3,1,2,0:T(8,128)S(1)}, u32[]{:S(2)}, u32[]{:S(2)}) %collective-permute-start.22) | collective-permute-done | bytes 12416 | tf_op jit(solution)/shard_map/ppermute | solution.py:20
  212.2 1.9 collective-permute-start.23
  214.1 7.2 %collective-permute-done.23 = f32[3,8,32,1]{3,2,1,0:T(8,128)S(1)} collective-permute-done((f32[3,8,32,1]{3,2,1,0:T(8,128)S(1)}, f32[3,8,32,1]{3,2,1,0:T(8,128)S(1)}, u32[]{:S(2)}, u32[]{:S(2)}) %collective-permute-start.23) | collective-permute-done | bytes 3104 | tf_op jit(solution)/shard_map/ppermute | solution.py:20
  (162 shorter events, 18.6 us)
Async XLA Ops:
  2.8 6.5 %collective-permute-start = (f32[6,1,32,128]{3,2,1,0:T(8,128)S(1)}, f32[6,1,32,128]{3,2,1,0:T(8,128)S(1)}, u32[]{:S(2)}, u32[]{:S(2)}) collective-permute-start(f32[6,1,32,128]{3,2,1,0:T(8,128)S(1)} %slice.632), channel_id=1, source_target_pairs={{8,0},{16,8},{24,16},{9,1},{17,9},{25,17},{10,2},{18,10},{26,18},{... | collective-permute-start | bytes 294920 | tf_op jit(solution)/shard_map/ppermute | solution.py:20
  5.5 44.0 %copy-start.4 = (f32[8,32,128]{2,1,0:T(8,128)}, f32[8,32,128]{2,1,0:T(8,128)S(1)}, u32[]{:S(2)}) copy-start(f32[8,32,128]{2,1,0:T(8,128)S(1)} %select_reduce_fusion) | copy-start | bytes 393220
  9.3 4.0 %collective-permute-start.1 = (f32[6,9,1,128]{3,2,1,0:T(1,128)S(1)}, f32[6,9,1,128]{3,2,1,0:T(1,128)S(1)}, u32[]{:S(2)}, u32[]{:S(2)}) collective-permute-start(f32[6,9,1,128]{3,2,1,0:T(1,128)S(1)} %pad_maximum_fusion.66), channel_id=1, source_target_pairs={{4,0},{5,1},{6,2},{7,3},{12,8},{13,9},{14,10},{15,11},{20,16},{21,... | collective-permute-start | bytes 82952 | tf_op jit(solution)/shard_map/ppermute | solution.py:20
  11.8 36.5 %copy-start.24 = (pred[8]{0:T(512)(128)(4,1)}, pred[8]{0:T(512)(128)(4,1)S(1)}, u32[]{:S(2)}) copy-start(pred[8]{0:T(512)(128)(4,1)S(1)} %get-tuple-element.167) | copy-start | bytes 28
  11.8 36.5 %copy-start.26 = (pred[8]{0:T(512)(128)(4,1)}, pred[8]{0:T(512)(128)(4,1)S(1)}, u32[]{:S(2)}) copy-start(pred[8]{0:T(512)(128)(4,1)S(1)} %get-tuple-element.168) | copy-start | bytes 28
  13.9 3.5 %collective-permute-start.2 = (f32[6,9,33,1]{2,3,1,0:T(1,128)S(1)}, f32[6,9,33,1]{2,3,1,0:T(1,128)S(1)}, u32[]{:S(2)}, u32[]{:S(2)}) collective-permute-start(f32[6,9,33,1]{2,3,1,0:T(1,128)S(1)} %copy.54), channel_id=1, source_target_pairs={{1,0},{2,1},{3,2},{5,4},{6,5},{7,6},{9,8},{10,9},{11,10},{13,12},{... | collective-permute-start | bytes 21392 | tf_op jit(solution)/shard_map/ppermute | solution.py:20
  15.8 32.5 %copy-start.28 = (pred[32]{0:T(512)(128)(4,1)}, pred[32]{0:T(512)(128)(4,1)S(1)}, u32[]{:S(2)}) copy-start(pred[32]{0:T(512)(128)(4,1)S(1)} %get-tuple-element.165) | copy-start | bytes 100
  15.8 32.5 %copy-start.30 = (pred[32]{0:T(512)(128)(4,1)}, pred[32]{0:T(512)(128)(4,1)S(1)}, u32[]{:S(2)}) copy-start(pred[32]{0:T(512)(128)(4,1)S(1)} %get-tuple-element.166) | copy-start | bytes 100
  22.6 26.9 %copy-start.2 = (f32[8,32,128]{2,1,0:T(8,128)}, f32[8,32,128]{2,1,0:T(8,128)S(1)}, u32[]{:S(2)}) copy-start(f32[8,32,128]{2,1,0:T(8,128)S(1)} %get-tuple-element.30) | copy-start | bytes 393220
  22.6 26.9 %copy-start.8 = (f32[8,32,128]{2,1,0:T(8,128)}, f32[8,32,128]{2,1,0:T(8,128)S(1)}, u32[]{:S(2)}) copy-start(f32[8,32,128]{2,1,0:T(8,128)S(1)} %get-tuple-element.37) | copy-start | bytes 393220
  22.6 25.7 %copy-start.6 = (f32[8,32,128]{2,1,0:T(8,128)S(1)}, f32[8,32,128]{2,1,0:T(8,128)}, u32[]{:S(2)}) copy-start(f32[8,32,128]{2,1,0:T(8,128)} %param.10) | copy-start | bytes 393220
  22.7 25.7 %copy-start.10 = (f32[8,32,128]{2,1,0:T(8,128)S(1)}, f32[8,32,128]{2,1,0:T(8,128)}, u32[]{:S(2)}) copy-start(f32[8,32,128]{2,1,0:T(8,128)} %param.9) | copy-start | bytes 393220
  22.7 6.0 %collective-permute-start.4 = (f32[1,32,128]{2,1,0:T(8,128)S(1)}, f32[1,32,128]{2,1,0:T(8,128)S(1)}, u32[]{:S(2)}, u32[]{:S(2)}) collective-permute-start(f32[1,32,128]{2,1,0:T(8,128)S(1)} %get-tuple-element.155), channel_id=1, source_target_pairs={{0,8},{8,16},{16,24},{1,9},{9,17},{17,25},{2,10},{10,18},{18,26},{... | collective-permute-start | bytes 49160 | tf_op jit(solution)/shard_map/ppermute | solution.py:28
  26.3 5.6 %collective-permute-start.3 = (f32[1,32,128]{2,1,0:T(8,128)S(1)}, f32[1,32,128]{2,1,0:T(8,128)S(1)}, u32[]{:S(2)}, u32[]{:S(2)}) collective-permute-start(f32[1,32,128]{2,1,0:T(8,128)S(1)} %get-tuple-element.156), channel_id=1, source_target_pairs={{8,0},{16,8},{24,16},{9,1},{17,9},{25,17},{10,2},{18,10},{26,18},{... | collective-permute-start | bytes 49160 | tf_op jit(solution)/shard_map/ppermute | solution.py:31
  32.0 7.1 %collective-permute-start.6 = (f32[10,1,128]{2,1,0:T(1,128)S(1)}, f32[10,1,128]{2,1,0:T(1,128)S(1)}, u32[]{:S(2)}, u32[]{:S(2)}) collective-permute-start(f32[10,1,128]{2,1,0:T(1,128)S(1)} %get-tuple-element.112), channel_id=1, source_target_pairs={{0,4},{1,5},{2,6},{3,7},{8,12},{9,13},{10,14},{11,15},{16,20},{17,... | collective-permute-start | bytes 15368 | tf_op jit(solution)/shard_map/ppermute | solution.py:28
  33.3 5.9 %collective-permute-start.5 = (f32[10,1,128]{2,1,0:T(1,128)S(1)}, f32[10,1,128]{2,1,0:T(1,128)S(1)}, u32[]{:S(2)}, u32[]{:S(2)}) collective-permute-start(f32[10,1,128]{2,1,0:T(1,128)S(1)} %get-tuple-element.113), channel_id=1, source_target_pairs={{4,0},{5,1},{6,2},{7,3},{12,8},{13,9},{14,10},{15,11},{20,16},{21,... | collective-permute-start | bytes 15368 | tf_op jit(solution)/shard_map/ppermute | solution.py:31
  39.3 6.8 %collective-permute-start.7 = (f32[10,34,1]{2,1,0:T(8,128)S(1)}, f32[10,34,1]{2,1,0:T(8,128)S(1)}, u32[]{:S(2)}, u32[]{:S(2)}) collective-permute-start(f32[10,34,1]{2,1,0:T(8,128)S(1)} %get-tuple-element.108), channel_id=1, source_target_pairs={{1,0},{2,1},{3,2},{5,4},{6,5},{7,6},{9,8},{10,9},{11,10},{13,12},{... | collective-permute-start | bytes 4088 | tf_op jit(solution)/shard_map/ppermute | solution.py:31
  41.2 7.1 %collective-permute-start.8 = (f32[10,34,1]{2,1,0:T(8,128)S(1)}, f32[10,34,1]{2,1,0:T(8,128)S(1)}, u32[]{:S(2)}, u32[]{:S(2)}) collective-permute-start(f32[10,34,1]{2,1,0:T(8,128)S(1)} %get-tuple-element.109), channel_id=1, source_target_pairs={{0,1},{1,2},{2,3},{4,5},{5,6},{6,7},{8,9},{9,10},{10,11},{12,13},{... | collective-permute-start | bytes 4088 | tf_op jit(solution)/shard_map/ppermute | solution.py:28
  43.6 63.5 %copy-start.18 = (pred[8]{0:T(512)(128)(4,1)}, pred[8]{0:T(512)(128)(4,1)S(1)}, u32[]{:S(2)}) copy-start(pred[8]{0:T(512)(128)(4,1)S(1)} %and_or_fusion.2) | copy-start | bytes 28
  52.0 7.2 %collective-permute-start.9 = (f32[4,1,33,129]{3,2,1,0:T(8,128)S(1)}, f32[4,1,33,129]{3,2,1,0:T(8,128)S(1)}, u32[]{:S(2)}, u32[]{:S(2)}) collective-permute-start(f32[4,1,33,129]{3,2,1,0:T(8,128)S(1)} %slice.669), channel_id=1, source_target_pairs={{0,8},{8,16},{16,24},{1,9},{9,17},{17,25},{2,10},{10,18},{18,26},{... | collective-permute-start | bytes 204344 | tf_op jit(solution)/shard_map/ppermute | solution.py:20
  53.9 53.2 %copy-start.20 = (pred[32]{0:T(512)(128)(4,1)}, pred[32]{0:T(512)(128)(4,1)S(1)}, u32[]{:S(2)}) copy-start(pred[32]{0:T(512)(128)(4,1)S(1)} %and_or_fusion.1) | copy-start | bytes 100
  59.4 5.8 %collective-permute-start.10 = (f32[4,8,1,129]{3,1,2,0:T(8,128)S(1)}, f32[4,8,1,129]{3,1,2,0:T(8,128)S(1)}, u32[]{:S(2)}, u32[]{:S(2)}) collective-permute-start(f32[4,8,1,129]{3,1,2,0:T(8,128)S(1)} %pad_maximum_fusion.64), channel_id=1, source_target_pairs={{0,4},{1,5},{2,6},{3,7},{8,12},{9,13},{10,14},{11,15},{16,20},{17,... | collective-permute-start | bytes 49544 | tf_op jit(solution)/shard_map/ppermute | solution.py:20
  65.3 41.4 %collective-permute-start.11 = (f32[4,8,32,1]{3,2,1,0:T(8,128)S(1)}, f32[4,8,32,1]{3,2,1,0:T(8,128)S(1)}, u32[]{:S(2)}, u32[]{:S(2)}) collective-permute-start(f32[4,8,32,1]{3,2,1,0:T(8,128)S(1)} %fusion.7), channel_id=1, source_target_pairs={{0,1},{1,2},{2,3},{4,5},{5,6},{6,7},{8,9},{9,10},{10,11},{12,13},{... | collective-permute-start | bytes 12296 | tf_op jit(solution)/shard_map/ppermute | solution.py:20
  67.3 39.9 %copy-start.22 = (pred[128]{0:T(512)(128)(4,1)}, pred[128]{0:T(512)(128)(4,1)S(1)}, u32[]{:S(2)}) copy-start(pred[128]{0:T(512)(128)(4,1)S(1)} %and_or_fusion) | copy-start | bytes 388
  107.7 6.5 %collective-permute-start.12 = (f32[6,1,32,128]{3,2,1,0:T(8,128)S(1)}, f32[6,1,32,128]{3,2,1,0:T(8,128)S(1)}, u32[]{:S(2)}, u32[]{:S(2)}) collective-permute-start(f32[6,1,32,128]{3,2,1,0:T(8,128)S(1)} %pad_maximum_fusion.61), channel_id=1, source_target_pairs={{8,0},{16,8},{24,16},{9,1},{17,9},{25,17},{10,2},{18,10},{26,18},{... | collective-permute-start | bytes 294920 | tf_op jit(solution)/shard_map/ppermute | solution.py:20
  114.2 4.9 %collective-permute-start.13 = (f32[6,9,1,128]{3,2,1,0:T(1,128)S(1)}, f32[6,9,1,128]{3,2,1,0:T(1,128)S(1)}, u32[]{:S(2)}, u32[]{:S(2)}) collective-permute-start(f32[6,9,1,128]{3,2,1,0:T(1,128)S(1)} %pad_maximum_fusion.65), channel_id=1, source_target_pairs={{4,0},{5,1},{6,2},{7,3},{12,8},{13,9},{14,10},{15,11},{20,16},{21,... | collective-permute-start | bytes 82952 | tf_op jit(solution)/shard_map/ppermute | solution.py:20
  119.7 3.5 %collective-permute-start.14 = (f32[6,9,33,1]{2,3,1,0:T(1,128)S(1)}, f32[6,9,33,1]{2,3,1,0:T(1,128)S(1)}, u32[]{:S(2)}, u32[]{:S(2)}) collective-permute-start(f32[6,9,33,1]{2,3,1,0:T(1,128)S(1)} %copy.55), channel_id=1, source_target_pairs={{1,0},{2,1},{3,2},{5,4},{6,5},{7,6},{9,8},{10,9},{11,10},{13,12},{... | collective-permute-start | bytes 21392 | tf_op jit(solution)/shard_map/ppermute | solution.py:20
  126.6 24.8 %copy-start.3 = (f32[8,32,128]{2,1,0:T(8,128)S(1)}, f32[8,32,128]{2,1,0:T(8,128)}, u32[]{:S(2)}) copy-start(f32[8,32,128]{2,1,0:T(8,128)} %copy-done.2) | copy-start | bytes 393220
  126.7 24.8 %copy-start.5 = (f32[8,32,128]{2,1,0:T(8,128)S(1)}, f32[8,32,128]{2,1,0:T(8,128)}, u32[]{:S(2)}) copy-start(f32[8,32,128]{2,1,0:T(8,128)} %copy-done.4) | copy-start | bytes 393220
  126.7 24.8 %copy-start.7 = (f32[8,32,128]{2,1,0:T(8,128)S(1)}, f32[8,32,128]{2,1,0:T(8,128)}, u32[]{:S(2)}) copy-start(f32[8,32,128]{2,1,0:T(8,128)} %param.10) | copy-start | bytes 393220
  126.7 24.8 %copy-start.9 = (f32[8,32,128]{2,1,0:T(8,128)S(1)}, f32[8,32,128]{2,1,0:T(8,128)}, u32[]{:S(2)}) copy-start(f32[8,32,128]{2,1,0:T(8,128)} %copy-done.8) | copy-start | bytes 393220
  126.7 24.8 %copy-start.11 = (f32[8,32,128]{2,1,0:T(8,128)S(1)}, f32[8,32,128]{2,1,0:T(8,128)}, u32[]{:S(2)}) copy-start(f32[8,32,128]{2,1,0:T(8,128)} %param.9) | copy-start | bytes 393220
  126.7 24.8 %copy-start.13 = (f32[8,32,128]{2,1,0:T(8,128)S(1)}, f32[8,32,128]{2,1,0:T(8,128)}, u32[]{:S(2)}) copy-start(f32[8,32,128]{2,1,0:T(8,128)} %copy-done.12) | copy-start | bytes 393220
  126.7 24.8 %copy-start.25 = (pred[8]{0:T(512)(128)(4,1)S(1)}, pred[8]{0:T(512)(128)(4,1)}, u32[]{:S(2)}) copy-start(pred[8]{0:T(512)(128)(4,1)} %copy-done.24) | copy-start | bytes 28
  126.7 24.8 %copy-start.27 = (pred[8]{0:T(512)(128)(4,1)S(1)}, pred[8]{0:T(512)(128)(4,1)}, u32[]{:S(2)}) copy-start(pred[8]{0:T(512)(128)(4,1)} %copy-done.26) | copy-start | bytes 28
  126.7 24.8 %copy-start.29 = (pred[32]{0:T(512)(128)(4,1)S(1)}, pred[32]{0:T(512)(128)(4,1)}, u32[]{:S(2)}) copy-start(pred[32]{0:T(512)(128)(4,1)} %copy-done.28) | copy-start | bytes 100
  126.7 24.8 %copy-start.31 = (pred[32]{0:T(512)(128)(4,1)S(1)}, pred[32]{0:T(512)(128)(4,1)}, u32[]{:S(2)}) copy-start(pred[32]{0:T(512)(128)(4,1)} %copy-done.30) | copy-start | bytes 100
  126.8 24.8 %copy-start.33 = (pred[128]{0:T(512)(128)(4,1)S(1)}, pred[128]{0:T(512)(128)(4,1)}, u32[]{:S(2)}) copy-start(pred[128]{0:T(512)(128)(4,1)} %copy-done.32) | copy-start | bytes 388
  126.8 24.8 %copy-start.35 = (pred[128]{0:T(512)(128)(4,1)S(1)}, pred[128]{0:T(512)(128)(4,1)}, u32[]{:S(2)}) copy-start(pred[128]{0:T(512)(128)(4,1)} %copy-done.34) | copy-start | bytes 388
  126.8 6.0 %collective-permute-start.16 = (f32[1,32,128]{2,1,0:T(8,128)S(1)}, f32[1,32,128]{2,1,0:T(8,128)S(1)}, u32[]{:S(2)}, u32[]{:S(2)}) collective-permute-start(f32[1,32,128]{2,1,0:T(8,128)S(1)} %get-tuple-element.130), channel_id=1, source_target_pairs={{0,8},{8,16},{16,24},{1,9},{9,17},{17,25},{2,10},{10,18},{18,26},{... | collective-permute-start | bytes 49160 | tf_op jit(solution)/shard_map/ppermute | solution.py:28
  129.5 5.6 %collective-permute-start.15 = (f32[1,32,128]{2,1,0:T(8,128)S(1)}, f32[1,32,128]{2,1,0:T(8,128)S(1)}, u32[]{:S(2)}, u32[]{:S(2)}) collective-permute-start(f32[1,32,128]{2,1,0:T(8,128)S(1)} %get-tuple-element.131), channel_id=1, source_target_pairs={{8,0},{16,8},{24,16},{9,1},{17,9},{25,17},{10,2},{18,10},{26,18},{... | collective-permute-start | bytes 49160 | tf_op jit(solution)/shard_map/ppermute | solution.py:31
  135.1 5.9 %collective-permute-start.18 = (f32[10,1,128]{2,1,0:T(1,128)S(1)}, f32[10,1,128]{2,1,0:T(1,128)S(1)}, u32[]{:S(2)}, u32[]{:S(2)}) collective-permute-start(f32[10,1,128]{2,1,0:T(1,128)S(1)} %get-tuple-element.110), channel_id=1, source_target_pairs={{0,4},{1,5},{2,6},{3,7},{8,12},{9,13},{10,14},{11,15},{16,20},{17,... | collective-permute-start | bytes 15368 | tf_op jit(solution)/shard_map/ppermute | solution.py:28
  136.4 5.9 %collective-permute-start.17 = (f32[10,1,128]{2,1,0:T(1,128)S(1)}, f32[10,1,128]{2,1,0:T(1,128)S(1)}, u32[]{:S(2)}, u32[]{:S(2)}) collective-permute-start(f32[10,1,128]{2,1,0:T(1,128)S(1)} %get-tuple-element.111), channel_id=1, source_target_pairs={{4,0},{5,1},{6,2},{7,3},{12,8},{13,9},{14,10},{15,11},{20,16},{21,... | collective-permute-start | bytes 15368 | tf_op jit(solution)/shard_map/ppermute | solution.py:31
  142.5 5.2 %collective-permute-start.19 = (f32[10,34,1]{2,1,0:T(8,128)S(1)}, f32[10,34,1]{2,1,0:T(8,128)S(1)}, u32[]{:S(2)}, u32[]{:S(2)}) collective-permute-start(f32[10,34,1]{2,1,0:T(8,128)S(1)} %get-tuple-element.106), channel_id=1, source_target_pairs={{1,0},{2,1},{3,2},{5,4},{6,5},{7,6},{9,8},{10,9},{11,10},{13,12},{... | collective-permute-start | bytes 4088 | tf_op jit(solution)/shard_map/ppermute | solution.py:31
  144.4 7.1 %collective-permute-start.20 = (f32[10,34,1]{2,1,0:T(8,128)S(1)}, f32[10,34,1]{2,1,0:T(8,128)S(1)}, u32[]{:S(2)}, u32[]{:S(2)}) collective-permute-start(f32[10,34,1]{2,1,0:T(8,128)S(1)} %get-tuple-element.107), channel_id=1, source_target_pairs={{0,1},{1,2},{2,3},{4,5},{5,6},{6,7},{8,9},{9,10},{10,11},{12,13},{... | collective-permute-start | bytes 4088 | tf_op jit(solution)/shard_map/ppermute | solution.py:28
  199.4 6.8 %collective-permute-start.21 = (f32[3,1,33,129]{3,2,1,0:T(8,128)S(1)}, f32[3,1,33,129]{3,2,1,0:T(8,128)S(1)}, u32[]{:S(2)}, u32[]{:S(2)}) collective-permute-start(f32[3,1,33,129]{3,2,1,0:T(8,128)S(1)} %slice.716), channel_id=1, source_target_pairs={{0,8},{8,16},{16,24},{1,9},{9,17},{17,25},{2,10},{10,18},{18,26},{... | collective-permute-start | bytes 153260 | tf_op jit(solution)/shard_map/ppermute | solution.py:20
  206.4 5.7 %collective-permute-start.22 = (f32[3,8,1,129]{3,1,2,0:T(8,128)S(1)}, f32[3,8,1,129]{3,1,2,0:T(8,128)S(1)}, u32[]{:S(2)}, u32[]{:S(2)}) collective-permute-start(f32[3,8,1,129]{3,1,2,0:T(8,128)S(1)} %pad_maximum_fusion.67), channel_id=1, source_target_pairs={{0,4},{1,5},{2,6},{3,7},{8,12},{9,13},{10,14},{11,15},{16,20},{17,... | collective-permute-start | bytes 37160 | tf_op jit(solution)/shard_map/ppermute | solution.py:20
  212.2 9.1 %collective-permute-start.23 = (f32[3,8,32,1]{3,2,1,0:T(8,128)S(1)}, f32[3,8,32,1]{3,2,1,0:T(8,128)S(1)}, u32[]{:S(2)}, u32[]{:S(2)}) collective-permute-start(f32[3,8,32,1]{3,2,1,0:T(8,128)S(1)} %fusion.11), channel_id=1, source_target_pairs={{0,1},{1,2},{2,3},{4,5},{5,6},{6,7},{8,9},{9,10},{10,11},{12,13},{... | collective-permute-start | bytes 9224 | tf_op jit(solution)/shard_map/ppermute | solution.py:20
  (13 other events, 71.2 us)
where the time goes:
time: 224 us; the launch traced here: 223 us
  blocking collectives  80.9 us (36%)
  starting transfers between devices  58.9 us (26%)
  waiting for transfers between devices  49.5 us (22%)
  other arithmetic  18.4 us (8%)
  local copies, waits for them, and re-layouts  8.76 us (4%)
  between operations  6.71 us (3%)
    pmin x2, blocking collectives, body(): time_step = COURANT * lax.pmin(jnp.min(step_ratio), ('gx', 'gy', 'gz'))  80.9 us
    ppermute x12, waiting for transfers between devices, passed_along(): lax.ppermute(value, axis, [(source, source + steps) for source in range(f...  35.8 us
    ppermute x12, starting transfers between devices, passed_along(): lax.ppermute(value, axis, [(source, source + steps) for source in range(f...  26.6 us
    ppermute x6, starting transfers between devices, extended_2(): lax.ppermute(lax.slice_in_dim(block, 0, width, axis=dim), axis, backward)  18.6 us
    ppermute x6, starting transfers between devices, extended_2(): lax.ppermute(lax.slice_in_dim(block, block.shape[dim] - width, None, axis...  13.7 us
    ppermute x6, waiting for transfers between devices, extended_2(): lax.ppermute(lax.slice_in_dim(block, 0, width, axis=dim), axis, backward)  7.75 us
    ppermute x6, waiting for transfers between devices, extended_2(): lax.ppermute(lax.slice_in_dim(block, block.shape[dim] - width, None, axis...  6.03 us
  transfers between devices with their start and end apart: 24, of which 17 were waited for; matrix products, arithmetic and copies ran while one was open for 1% of the time, Pallas kernels for 0%

commit v1 on v0

v1 whole, which is shorter than its diff:
```python
import functools

import jax
import jax.numpy as jnp
from jax import lax
from jax.experimental import pallas as pl
from jax.experimental.pallas import tpu as pltpu
from jax.sharding import PartitionSpec as P

STEPS = 2
COURANT = 0.25
MESH = pl.DeviceIdType.MESH
AXES = ("gx", "gy", "gz")
ROWS = 8


def up8(n):
    return -(-n // 8) * 8


def kernel(sizes, shape, adi, flags, d_ref, v_ref, e_ref, rho_ref, reg_ref,
           do_ref, vo_ref, eo_ref,
           N, SYA, RYA, SZA, G, GS, T, C, VOL, GAM, ER, MA, R, SYB, RYB, SZB, RZB,
           SZC, RZC, F, SYC, RYC, RXC, INVM, ACC, SZD, RZD, DS, DRX, DRY, DRZ,
           ssem, rsem):
    X, Y, Z = shape
    XN, YN, YP = X + 1, Y + 1, Y + 8
    n_of = dict(zip(AXES, sizes))
    me = {a: lax.axis_index(a) for a in AXES}
    first = {a: me[a] == 0 for a in AXES}
    last = {a: me[a] == n_of[a] - 1 for a in AXES}
    count = [0]
    pending = []

    def remote(src, dst, axis, target):
        k = count[0]
        count[0] += 1
        return pltpu.make_async_remote_copy(
            src_ref=src, dst_ref=dst, send_sem=ssem.at[k], recv_sem=rsem.at[k],
            device_id={axis: target}, device_id_type=MESH)

    def shift(src, dst, axis, step):
        can_send = jnp.logical_not(last[axis] if step == 1 else first[axis])
        can_recv = jnp.logical_not(first[axis] if step == 1 else last[axis])
        target = jnp.clip(me[axis] + step, 0, n_of[axis] - 1)
        copy = remote(src, dst, axis, target)

        @pl.when(can_send)
        def _():
            copy.start()

        def drain():
            @pl.when(can_send)
            def _():
                copy.wait_send()

        pending.append(drain)

        def arrived():
            @pl.when(can_recv)
            def _():
                copy.wait_recv()

        return arrived

    def spread_min(tile, s, slot, axis, buf):
        n = n_of[axis]
        DS[s, slot] = tile
        copies = []
        for off in range(1, n):
            copy = remote(DS.at[s, slot], buf.at[s, off - 1], axis, lax.rem(me[axis] + off, n))
            copy.start()
            pending.append(copy.wait_send)
            copies.append(copy)

        def result():
            out = tile
            for off, copy in enumerate(copies):
                copy.wait_recv()
                out = jnp.minimum(out, buf[s, off])
            return out

        return result

    def loop(n, f):
        def step(i, carry):
            f(i)
            return carry
        lax.fori_loop(0, n, step, 0)

    barrier = pltpu.get_barrier_semaphore()
    total = 0
    for a in AXES:
        for off in range(1, n_of[a]):
            pl.semaphore_signal(barrier, inc=1,
                                device_id={a: lax.rem(me[a] + off, n_of[a])},
                                device_id_type=MESH)
            total += 1
    pl.semaphore_wait(barrier, total)

    wait_d = shift(d_ref.at[:, 0], N.at[0:3, X, 0:Y], "gx", -1)
    wait_v = shift(v_ref.at[:, 0], N.at[3:6, X, 0:Y], "gx", -1)

    lane = lax.broadcasted_iota(jnp.int32, (Y, Z), 1)
    lane_p = lax.broadcasted_iota(jnp.int32, (YP, Z), 1)
    row_p = lax.broadcasted_iota(jnp.int32, (YP, Z), 0)
    row = lax.broadcasted_iota(jnp.int32, (Y, Z), 0)
    lane_b = lax.broadcasted_iota(jnp.int32, (ROWS, Z), 1)
    row_b = lax.broadcasted_iota(jnp.int32, (ROWS, Z), 0)
    i32 = lambda b: b.astype(jnp.int32)
    far = 1 << 20
    end_x = jnp.where(last["gx"], X - 1, far)
    end_y = jnp.where(last["gy"], Y - 1, far)
    end_z = jnp.where(last["gz"], Z - 1, far)
    start_x = jnp.where(first["gx"], 0, far)
    start_y = jnp.where(first["gy"], 0, far)
    start_z = jnp.where(first["gz"], 0, far)

    def present_of(i, r0):
        edge = jnp.where(i == end_x, -1, 0)
        rb = row_b + r0
        inside = jnp.where((rb == end_y) | (lane_b == end_z), -1, 0)
        return (inside + edge) == 0

    zeros_p = jnp.zeros((YP, Z), jnp.float32)

    @pl.when(last["gx"])
    def _():
        for c in range(6):
            N[c, X] = zeros_p
        for s in range(STEPS):
            R[s, X + 1] = jnp.zeros(R.shape[2:], jnp.float32)
            for c in range(4):
                RXC[s, 1, c] = zeros_p

    @pl.when(first["gx"])
    def _():
        for s in range(STEPS):
            R[s, 0] = jnp.zeros(R.shape[2:], jnp.float32)
            for c in range(4):
                RXC[s, 0, c] = zeros_p

    @pl.when(last["gy"])
    def _():
        RYA[...] = jnp.zeros(RYA.shape, jnp.float32)
        for s in range(STEPS):
            RYB[s, 1] = jnp.zeros(RYB.shape[2:], jnp.float32)
            RYC[s, 1] = jnp.zeros(RYC.shape[2:], jnp.float32)

    @pl.when(first["gy"])
    def _():
        for s in range(STEPS):
            RYB[s, 0] = jnp.zeros(RYB.shape[2:], jnp.float32)
            RYC[s, 0] = jnp.zeros(RYC.shape[2:], jnp.float32)

    @pl.when(last["gz"])
    def _():
        G[...] = zeros_p
        RZD[...] = zeros_p
        for s in range(STEPS):
            RZB[s, 1] = jnp.zeros((Y, Z), jnp.float32)

    @pl.when(first["gz"])
    def _():
        for s in range(STEPS):
            RZB[s, 0] = jnp.zeros((Y, Z), jnp.float32)
            RZC[s] = jnp.zeros((Y, Z), jnp.float32)

    def load(i):
        for c in range(3):
            N[c, i, 0:Y] = d_ref[c, i]
            N[3 + c, i, 0:Y] = v_ref[c, i]
        reg = reg_ref[i]
        gam = jnp.zeros((Y, Z), jnp.float32)
        for k in range(adi.shape[0]):
            gam = jnp.where(reg == k, adi[k], gam)
        GAM[i] = gam
        for r0 in range(0, Y, ROWS):
            rs = slice(r0, r0 + ROWS)
            MA[i, rs] = jnp.where(present_of(i, r0), 0.125 * rho_ref[i, rs], 0.0)

    loop(X, load)

    wait_d()
    wait_v()
    for c in range(6):
        for i in range(XN):
            SYA[c * XN + i:c * XN + i + 1] = N[c, i, 0:1]
    wait = shift(SYA, RYA, "gy", -1)
    wait()
    for c in range(6):
        for i in range(XN):
            N[c, i, Y:YN] = RYA[c * XN + i:c * XN + i + 1]
    packed = zeros_p
    for c in range(6):
        for i in range(XN):
            j = c * XN + i
            value = N[c, i]
            packed = jnp.where(lane_p == j, pltpu.roll(value, j, 1) if j else value, packed)
    SZA[...] = packed
    wait = shift(SZA, G, "gz", -1)
    wait()

    for s in range(STEPS):
        final = s == STEPS - 1
        energy_ref = e_ref if s == 0 else eo_ref

        GS[0] = G[0:Y] + G[1:YN]
        GS[1] = G[1:YN] - G[0:Y]

        def plane_sums(i):
            for c in range(6):
                back = Z - 1 - (c * XN + i)
                ghost_s = pltpu.roll(GS[0], back, 1)
                ghost_d = pltpu.roll(GS[1], back, 1)
                low, high = N[c, i, 0:Y], N[c, i, 1:YN]
                ys, yd = low + high, high - low
                ys1 = jnp.where(lane == Z - 1, ghost_s, pltpu.roll(ys, Z - 1, 1))
                yd1 = jnp.where(lane == Z - 1, ghost_d, pltpu.roll(yd, Z - 1, 1))
                T[3 * c, i] = ys + ys1
                T[3 * c + 1, i] = yd + yd1
                T[3 * c + 2, i] = ys1 - ys

        loop(XN, plane_sums)

        def kinematics(i):
            for r0 in range(0, Y, ROWS):
                rs = slice(r0, r0 + ROWS)

                def grad(c):
                    return (
                        0.25 * (T[3 * c, i + 1, rs] - T[3 * c, i, rs]),
                        0.25 * (T[3 * c + 1, i + 1, rs] + T[3 * c + 1, i, rs]),
                        0.25 * (T[3 * c + 2, i + 1, rs] + T[3 * c + 2, i, rs]),
                    )

                jac = [list(grad(c)) for c in range(3)]
                for c in range(3):
                    jac[c][c] = jac[c][c] + 1.0

                def minor(r1, r2, c1, c2):
                    return jac[r1][c1] * jac[r2][c2] - jac[r1][c2] * jac[r2][c1]

                cof = [
                    [minor(1, 2, 1, 2), minor(1, 2, 2, 0), minor(1, 2, 0, 1)],
                    [minor(2, 0, 1, 2), minor(2, 0, 2, 0), minor(2, 0, 0, 1)],
                    [minor(0, 1, 1, 2), minor(0, 1, 2, 0), minor(0, 1, 0, 1)],
                ]
                volume = jac[0][0] * cof[0][0] + jac[0][1] * cof[0][1] + jac[0][2] * cof[0][2]
                change = 0.0
                for c in range(3):
                    rate = grad(3 + c)
                    for e in range(3):
                        change = change + cof[c][e] * rate[e]
                        C[3 * c + e, i, rs] = cof[c][e]
                VOL[i, rs] = volume
                R[s, i + 1, 8 + r0:8 + r0 + ROWS] = change / volume

        loop(X, kinematics)

        own = slice(8, 8 + Y)
        waits = [
            shift(R.at[s, X, own], R.at[s, 0, own], "gx", 1),
            shift(R.at[s, 1, own], R.at[s, X + 1, own], "gx", -1),
        ]
        for i in range(X):
            SYB[s, 0, i:i + 1] = R[s, i + 1, 7 + Y:8 + Y]
            SYB[s, 1, i:i + 1] = R[s, i + 1, 8:9]
        waits += [
            shift(SYB.at[s, 0], RYB.at[s, 0], "gy", 1),
            shift(SYB.at[s, 1], RYB.at[s, 1], "gy", -1),
        ]
        to_up = to_down = jnp.zeros((Y, Z), jnp.float32)
        for i in range(X):
            value = R[s, i + 1, own]
            to_up = jnp.where(lane == i, pltpu.roll(value, i + 1, 1), to_up)
            to_down = jnp.where(lane == i, pltpu.roll(value, i, 1) if i else value, to_down)
        SZB[s, 0] = to_up
        SZB[s, 1] = to_down
        waits += [
            shift(SZB.at[s, 0], RZB.at[s, 0], "gz", 1),
            shift(SZB.at[s, 1], RZB.at[s, 1], "gz", -1),
        ]
        for w in waits:
            w()
        for i in range(X):
            R[s, i + 1, 7:8] = RYB[s, 0, i:i + 1]
            R[s, i + 1, 8 + Y:9 + Y] = RYB[s, 1, i:i + 1]

        is_one = [jnp.where(flags[k] == 1, 1.0, 0.0) for k in range(6)]

        def stresses(i, least):
            low_x, high_x = i == start_x, i == end_x - 1
            for r0 in range(0, Y, ROWS):
                rs = slice(r0, r0 + ROWS)
                rr = slice(8 + r0, 8 + r0 + ROWS)
                rate = R[s, i + 1, rr]
                rb = row_b + r0
                present = present_of(i, r0)
                xl = jnp.where(low_x, is_one[0] * rate, R[s, i, rr])
                xu = jnp.where(high_x, is_one[1] * rate, R[s, i + 2, rr])
                yl = jnp.where(rb == start_y, is_one[2] * rate,
                               R[s, i + 1, 7 + r0:7 + r0 + ROWS])
                yu = jnp.where(rb == end_y - 1, is_one[3] * rate,
                               R[s, i + 1, 9 + r0:9 + r0 + ROWS])
                ghost_l = pltpu.roll(RZB[s, 0, rs], lax.rem(Z - i, Z), 1)
                ghost_u = pltpu.roll(RZB[s, 1, rs], Z - 1 - i, 1)
                zl = jnp.where(lane_b == 0, ghost_l, pltpu.roll(rate, 1, 1))
                zu = jnp.where(lane_b == Z - 1, ghost_u, pltpu.roll(rate, Z - 1, 1))
                zl = jnp.where(lane_b == start_z, is_one[4] * rate, zl)
                zu = jnp.where(lane_b == end_z - 1, is_one[5] * rate, zu)
                rough = 0.0
                for lo, hi in ((xl, xu), (yl, yu), (zl, zu)):
                    f, g = hi - rate, rate - lo
                    rough = rough + jnp.abs(
                        jnp.maximum(jnp.minimum(f, g), 0.0) + jnp.minimum(jnp.maximum(f, g), 0.0))
                volume = VOL[i, rs]
                size = jnp.exp(jnp.log(jnp.abs(volume)) * (1.0 / 3.0))
                gam, energy = GAM[i, rs], energy_ref[i, rs]
                compress = jnp.maximum(-rate, 0.0)
                visc = size * size * compress * (compress + rough)
                ge = (gam - 1.0) * energy
                work = jnp.where(present, ge + visc, 0.0)
                signed = jnp.where(volume < 0.0, -size, size)
                ratio = signed * lax.rsqrt(gam * ge + visc)
                least = jnp.minimum(least, jnp.where(present, ratio, jnp.inf))
                ER[i, rs] = jnp.where(present, work * rate, 0.0)
                quarter = jnp.where(present, 0.25 * work * rho_ref[i, rs] / volume, 0.0)
                for q in range(9):
                    C[q, i, rs] = jnp.where(present, quarter * C[q, i, rs], 0.0)
            return least

        least = lax.fori_loop(0, X, stresses, jnp.full((ROWS, Z), jnp.inf, jnp.float32))

        min_z = spread_min(least, s, 0, "gz", DRZ)
        parts = 9 if s else 10

        def column_pack(i, packed):
            for q in range(parts):
                value = C[q, i] if q < 9 else MA[i]
                packed = jnp.where(lane == q * X + i, pltpu.roll(value, q * X + i + 1, 1), packed)
            return packed

        SZC[s] = lax.fori_loop(0, X, column_pack, jnp.zeros((Y, Z), jnp.float32))
        wait = shift(SZC.at[s], RZC.at[s], "gz", 1)
        wait()
        comps = 3 if s else 4
        for c in range(comps):
            F[s, c, 0] = zeros_p

        def node_sums(i):
            def below(q):
                value = C[q, i] if q < 9 else MA[i]
                ghost = pltpu.roll(RZC[s], lax.rem(Z - (q * X + i), Z), 1)
                return value, jnp.where(lane == 0, ghost, pltpu.roll(value, 1, 1))

            def rows_of(value):
                moved = pltpu.roll(value, 1, 0)
                return jnp.where(row == 0, 0.0, moved), moved[0:1]

            for c in range(comps):
                if c < 3:
                    a, a1 = below(3 * c)
                    p = a + a1
                    a, a1 = below(3 * c + 1)
                    q = a + a1
                    a, a1 = below(3 * c + 2)
                    r = a1 - a
                    pm, p_end = rows_of(p)
                    qm, q_end = rows_of(q)
                    rm, r_end = rows_of(r)
                    u, u_end = p + pm, p_end
                    v, v_end = (qm - q) + (r + rm), q_end + r_end
                    to_low, to_low_end = v - u, v_end - u_end
                    to_high, to_high_end = v + u, v_end + u_end
                else:
                    a, a1 = below(9)
                    p = a + a1
                    pm, p_end = rows_of(p)
                    to_low = to_high = p + pm
                    to_low_end = to_high_end = p_end
                F[s, c, i, 0:Y] = F[s, c, i, 0:Y] + to_low
                F[s, c, i, Y:YN] = F[s, c, i, Y:YN] + to_low_end
                F[s, c, i + 1, 0:Y] = to_high
                F[s, c, i + 1, Y:YN] = to_high_end

        loop(X, node_sums)

        min_y = spread_min(min_z(), s, 1, "gy", DRY)
        for c in range(comps):
            for i in range(XN):
                j = c * XN + i
                SYC[s, 0, j:j + 1] = F[s, c, i, Y:YN]
                if not final:
                    SYC[s, 1, j:j + 1] = F[s, c, i, 0:1]
        waits = [shift(SYC.at[s, 0], RYC.at[s, 0], "gy", 1)]
        if not final:
            waits.append(shift(SYC.at[s, 1], RYC.at[s, 1], "gy", -1))
        for w in waits:
            w()
        for c in range(comps):
            for i in range(XN):
                j = c * XN + i
                F[s, c, i, 0:1] = F[s, c, i, 0:1] + RYC[s, 0, j:j + 1]
                if not final:
                    F[s, c, i, Y:YN] = F[s, c, i, Y:YN] + RYC[s, 1, j:j + 1]

        waits = [shift(F.at[s, 0:comps, X], RXC.at[s, 0, 0:comps], "gx", 1)]
        if not final:
            waits.append(shift(F.at[s, 0:comps, 0], RXC.at[s, 1, 0:comps], "gx", -1))
        min_x = spread_min(min_y(), s, 2, "gx", DRX)
        for w in waits:
            w()

        def total_of(c, i):
            value = F[s, c, i]
            if isinstance(i, int) and i == 0:
                value = value + RXC[s, 0, c]
            if isinstance(i, int) and i == X and not final:
                value = value + RXC[s, 1, c]
            return value

        def accelerate(i):
            if s == 0:
                mass = total_of(3, i)
                inverse = jnp.where(mass > 0.0, 1.0 / mass, 0.0)
                INVM[i] = inverse
            else:
                inverse = INVM[i]
            for c in range(3):
                ACC[c, i] = total_of(c, i) * inverse

        for i in range(X if final else XN):
            accelerate(i)

        if not final:
            packed = zeros_p
            for c in range(3):
                for i in range(XN):
                    j = (3 + c) * XN + i
                    packed = jnp.where(lane_p == j, pltpu.roll(ACC[c, i], j, 1), packed)
            SZD[...] = packed
            wait = shift(SZD, RZD, "gz", -1)
        dt = COURANT * jnp.min(min_x())

        one = [flags[k] == 1 for k in range(6)]
        wall_x0 = jnp.where(one[0], start_x, far)
        wall_x1 = jnp.where(one[1], end_x, far)
        wall_y0 = jnp.where(one[2], start_y, far)
        wall_y1 = jnp.where(one[3], end_y, far)
        wall_z0 = jnp.where(one[4], start_z, far)
        wall_z1 = jnp.where(one[5], end_z, far)
        rows = Y if final else YP
        row_n, lane_n = (row, lane) if final else (row_p, lane_p)

        def move(i):
            for c in range(3):
                speed = N[3 + c, i, 0:rows] + dt * ACC[c, i, 0:rows]
                if c == 0:
                    on_wall = (i == wall_x0) | (i == wall_x1)
                elif c == 1:
                    on_wall = (row_n == wall_y0) | (row_n == wall_y1)
                else:
                    on_wall = (lane_n == wall_z0) | (lane_n == wall_z1)
                speed = jnp.where(on_wall, 0.0, speed)
                place = N[c, i, 0:rows] + dt * speed
                if final:
                    vo_ref[c, i] = speed
                    do_ref[c, i] = place
                else:
                    N[3 + c, i] = speed
                    N[c, i] = place

        loop(X if final else XN, move)

        def heat(i):
            eo_ref[i] = energy_ref[i] - dt * ER[i]

        loop(X, heat)

        if not final:
            wait()
            ghosts = G[...]
            speed = ghosts + dt * RZD[...]
            base = 3 * XN
            on_x = (lane_p == base + wall_x0) | (lane_p == base + wall_x1)
            on_y = (lane_p >= base + XN) & (lane_p < base + 2 * XN) & (
                (row_p == wall_y0) | (row_p == wall_y1))
            speed = jnp.where(on_x | on_y, 0.0, speed)
            place = ghosts + dt * pltpu.roll(speed, Z - base, 1)
            G[...] = jnp.where(lane_p < base, place, speed)

    for drain in pending:
        drain()


def solution(mesh):
    sizes = tuple(mesh.shape[a] for a in AXES)

    def body(displacement, velocity, energy, density, region, adiabatic, face_flags):
        X, Y, Z = shape = energy.shape
        XN, YP = X + 1, Y + 8
        f32 = jnp.float32
        vm = lambda *dims: pltpu.VMEM(dims, f32)
        copies = 4 + STEPS * (6 + 5 + sum(n - 1 for n in sizes)) + 1
        scratch = [
            vm(6, XN, YP, Z), vm(up8(6 * XN), Z), vm(up8(6 * XN), Z), vm(YP, Z), vm(YP, Z),
            vm(2, Y, Z), vm(18, XN, Y, Z), vm(9, X, Y, Z), vm(X, Y, Z), vm(X, Y, Z),
            vm(X, Y, Z), vm(X, Y, Z), vm(STEPS, X + 2, Y + 16, Z),
            vm(STEPS, 2, up8(X), Z), vm(STEPS, 2, up8(X), Z),
            vm(STEPS, 2, Y, Z), vm(STEPS, 2, Y, Z),
            vm(STEPS, Y, Z), vm(STEPS, Y, Z), vm(STEPS, 4, XN, YP, Z),
            vm(STEPS, 2, up8(4 * XN), Z), vm(STEPS, 2, up8(4 * XN), Z),
            vm(STEPS, 2, 4, YP, Z), vm(XN, YP, Z), vm(3, XN, YP, Z), vm(YP, Z), vm(YP, Z),
            vm(STEPS, 3, ROWS, Z),
            vm(STEPS, max(1, sizes[0] - 1), ROWS, Z),
            vm(STEPS, max(1, sizes[1] - 1), ROWS, Z),
            vm(STEPS, max(1, sizes[2] - 1), ROWS, Z),
            pltpu.SemaphoreType.DMA((copies,)), pltpu.SemaphoreType.DMA((copies,)),
        ]
        spec_v = pl.BlockSpec(memory_space=pltpu.VMEM)
        spec_s = pl.BlockSpec(memory_space=pltpu.SMEM)
        node = jax.ShapeDtypeStruct(displacement.shape, f32)
        return pl.pallas_call(
            functools.partial(kernel, sizes, shape),
            out_shape=(node, node, jax.ShapeDtypeStruct(energy.shape, f32)),
            in_specs=[spec_s, spec_s] + [spec_v] * 5,
            out_specs=(spec_v, spec_v, spec_v),
            scratch_shapes=scratch,
            compiler_params=pltpu.CompilerParams(
                collective_id=0, has_side_effects=True, vmem_limit_bytes=48 * 1024 * 1024),
        )(adiabatic, face_flags, displacement, velocity, energy, density, region)

    node = P(None, "gx", "gy", "gz")
    elem = P("gx", "gy", "gz")
    return jax.shard_map(
        body, mesh=mesh,
        in_specs=(node, node, elem, elem, elem, P(), P()),
        out_specs=(node, node, elem), check_vma=False)
```

time: 224 us -> 57.8 us (0.26)
  the two profiles are of different devices: /device:TPU:14 before, /device:TPU:0 now
where the time goes in v1:
time: 57.8 us; the launch traced here: 57.5 us
  Pallas kernels  48.7 us (84%)
  local copies, waits for them, and re-layouts  8.15 us (14%)
  between operations  0.66 us (1%)
    pallas_call x1, Pallas kernels, body(): pl.pallas_call(functools.partial(kernel, sizes, shape), out_shape=(node,...  48.7 us
    unnamed x17, local copies, waits for them, and re-layouts  8.15 us

profile of v1, /device:TPU:0, one launch (start us, length us, event | category | flops | bytes accessed | tf_op | source)
XLA Modules:
  0.0 57.5 jit_solution(4246259869540495068)
XLA Ops:
  0.6 0.0 copy-start
  0.6 1.0 %copy-done = f32[3,8,32,128]{3,2,1,0:T(8,128)S(1)} copy-done((f32[3,8,32,128]{3,2,1,0:T(8,128)S(1)}, f32[3,8,32,128]{3,2,1,0:T(8,128)}, u32[]{:S(2)}) %copy-start) | copy-done | bytes 393240
  1.6 0.0 copy-start.1
  1.6 1.0 %copy-done.1 = f32[3,8,32,128]{3,2,1,0:T(8,128)S(1)} copy-done((f32[3,8,32,128]{3,2,1,0:T(8,128)S(1)}, f32[3,8,32,128]{3,2,1,0:T(8,128)}, u32[]{:S(2)}) %copy-start.1) | copy-done | bytes 393240
  2.6 0.0 copy-start.2
  2.6 0.9 %copy-done.2 = f32[8,32,128]{2,1,0:T(8,128)S(1)} copy-done((f32[8,32,128]{2,1,0:T(8,128)S(1)}, f32[8,32,128]{2,1,0:T(8,128)}, u32[]{:S(2)}) %copy-start.2) | copy-done | bytes 131096
  3.5 0.0 copy-start.3
  3.5 0.9 %copy-done.3 = f32[8,32,128]{2,1,0:T(8,128)S(1)} copy-done((f32[8,32,128]{2,1,0:T(8,128)S(1)}, f32[8,32,128]{2,1,0:T(8,128)}, u32[]{:S(2)}) %copy-start.3) | copy-done | bytes 131096
  4.4 0.0 copy-start.4
  4.4 0.9 %copy-done.4 = s32[8,32,128]{2,1,0:T(8,128)S(1)} copy-done((s32[8,32,128]{2,1,0:T(8,128)S(1)}, s32[8,32,128]{2,1,0:T(8,128)}, u32[]{:S(2)}) %copy-start.4) | copy-done | bytes 131096
  5.3 0.0 copy-start.5
  5.3 0.7 %copy-done.5 = f32[11]{0:T(128)S(1)} copy-done((f32[11]{0:T(128)S(1)}, f32[11]{0:T(128)}, u32[]{:S(2)}) %copy-start.5) | copy-done | bytes 68
  6.0 0.0 copy-start.6
  6.0 0.7 %copy-done.6 = s32[6]{0:T(128)S(1)} copy-done((s32[6]{0:T(128)S(1)}, s32[6]{0:T(128)}, u32[]{:S(2)}) %copy-start.6) | copy-done | bytes 48
  6.7 48.7 %shard_map.94 = (f32[3,8,32,128]{3,2,1,0:T(8,128)S(1)}, f32[3,8,32,128]{3,2,1,0:T(8,128)S(1)}, f32[8,32,128]{2,1,0:T(8,128)S(1)}) custom-call(f32[11]{0:T(128)S(1)} %copy-done.5, s32[6]{0:T(128)S(1)} %copy-done.6, f32[3,8,32,128]{3,2,1,0:T(8,128)S(1)} %copy-done, f32[3,8,32,128]{3,2,1,0:T(8,128)S(1)} %copy-done.1, f32[8,32,128]{2,1,0:T(8,128)S(1)} %copy-done.2, ...), custom_call_target="tpu_custom_call" | custom-call | tf_op jit(solution)/shard_map/pallas_call | solution.py:524
  55.3 0.7 %copy.13 = f32[3,8,32,128]{3,2,1,0:T(8,128)} copy(f32[3,8,32,128]{3,2,1,0:T(8,128)S(1)} %get-tuple-element.6) | data formatting | bytes 786432
  56.1 0.7 %copy.14 = f32[3,8,32,128]{3,2,1,0:T(8,128)} copy(f32[3,8,32,128]{3,2,1,0:T(8,128)S(1)} %get-tuple-element.7) | data formatting | bytes 786432
  56.8 0.7 %copy.15 = f32[8,32,128]{2,1,0:T(8,128)} copy(f32[8,32,128]{2,1,0:T(8,128)S(1)} %get-tuple-element.8) | data formatting | bytes 262144
Async XLA Ops:
  0.6 1.0 %copy-start = (f32[3,8,32,128]{3,2,1,0:T(8,128)S(1)}, f32[3,8,32,128]{3,2,1,0:T(8,128)}, u32[]{:S(2)}) copy-start(f32[3,8,32,128]{3,2,1,0:T(8,128)} %d_ref.1) | copy-start | bytes 1179652
  1.6 1.0 %copy-start.1 = (f32[3,8,32,128]{3,2,1,0:T(8,128)S(1)}, f32[3,8,32,128]{3,2,1,0:T(8,128)}, u32[]{:S(2)}) copy-start(f32[3,8,32,128]{3,2,1,0:T(8,128)} %v_ref.1) | copy-start | bytes 1179652
  2.6 0.9 %copy-start.2 = (f32[8,32,128]{2,1,0:T(8,128)S(1)}, f32[8,32,128]{2,1,0:T(8,128)}, u32[]{:S(2)}) copy-start(f32[8,32,128]{2,1,0:T(8,128)} %e_ref.1) | copy-start | bytes 393220
  3.5 0.9 %copy-start.3 = (f32[8,32,128]{2,1,0:T(8,128)S(1)}, f32[8,32,128]{2,1,0:T(8,128)}, u32[]{:S(2)}) copy-start(f32[8,32,128]{2,1,0:T(8,128)} %rho_ref.1) | copy-start | bytes 393220
  4.4 0.9 %copy-start.4 = (s32[8,32,128]{2,1,0:T(8,128)S(1)}, s32[8,32,128]{2,1,0:T(8,128)}, u32[]{:S(2)}) copy-start(s32[8,32,128]{2,1,0:T(8,128)} %reg_ref.1) | copy-start | bytes 393220
  5.3 0.7 %copy-start.5 = (f32[11]{0:T(128)S(1)}, f32[11]{0:T(128)}, u32[]{:S(2)}) copy-start(f32[11]{0:T(128)} %adi.1) | copy-start | bytes 136
  6.0 0.7 %copy-start.6 = (s32[6]{0:T(128)S(1)}, s32[6]{0:T(128)}, u32[]{:S(2)}) copy-start(s32[6]{0:T(128)} %flags.1) | copy-start | bytes 76
